TPU v7x, 256 devices: a whole 4x4x8 slice. The times are simulated.
256 devices in a mesh: dp: 4 (over x_hi, core), ctx: 64 (over z, y, x_lo).
Axes of the slice: x: 4 (x_hi: 2, x_lo: 2; x = x_hi * 2 + x_lo), y: 4, z: 8, core: 2. Of those that a mesh axis runs over, the one named last changes fastest.
Arguments:
- queries: bfloat16 [4, 8192, 2560], P('dp', 'ctx'), may hold values from -6 to 6
- keys: bfloat16 [4, 8192, 512], P('dp', 'ctx'), may hold values from -6 to 6
- values: bfloat16 [4, 8192, 512], P('dp', 'ctx'), may hold values from -6 to 6
- out_grad: bfloat16 [4, 8192, 2560], P('dp', 'ctx'), may hold values from -24 to 24
- layer_input: bfloat16 [4, 8192, 5120], P('dp', 'ctx'), may hold values from -16 to 16
- doc_lens: int32 [4, 16], P('dp'), may hold values from 1 to 1024, 8192 in all within a row
Outputs:
- attn_out: bfloat16 [4, 8192, 2560], P('dp', 'ctx')
- query_grad: bfloat16 [4, 8192, 2560], P('dp', 'ctx')
- key_grad: bfloat16 [4, 8192, 512], P('dp', 'ctx')
- value_grad: bfloat16 [4, 8192, 512], P('dp', 'ctx')
- weight_grad: float32 [5120, 1024], P(('dp', 'ctx'))
Inputs may be any that keep to these rules, and one draw needn't show every extreme that they name: `doc_lens`: the documents of a micro-batch lie end to end and fill its 8192 positions; in every micro-batch the longest has exactly 1024 positions.
All inputs are finite; a program needn't handle non-finite values.
Results may differ from a plain program's by a relative error of at most 0.029.
Values may be sent and summed in bfloat16 or wider, within the bound.
No kernel may reach another device: no remote copies, remote signals or barrier semaphores. Data moves between devices by JAX's collectives and lax.ppermute only.
A program may use at most 128 MiB of HBM per device.

v0:
```python
import math
import jax
import jax.numpy as jnp
from jax import lax
from jax.sharding import Mesh
from jax.sharding import PartitionSpec as P

D = 5120
HD = 128
NEGATIVE = -1e30
CTX = ("cz", "cw")


def shifted(block, distance, n_ctx):
    route = [(i - distance, i) for i in range(n_ctx) if 0 <= i - distance < n_ctx]
    return lax.ppermute(block, CTX, route)


def doc_index(lengths_row, positions):
    bounds = jnp.cumsum(lengths_row)
    return jnp.sum((positions[:, None] >= bounds[None, :]).astype(jnp.int32), axis=1)


def make_shards(n_data, n_cz, n_cw):
    n_context = n_cz * n_cw

    def shards(queries, keys, values, out_grad, layer_input, doc_lens):
        tok_rows = queries.shape[1]
        kv_width = keys.shape[2]
        heads_kv = kv_width // HD
        group = queries.shape[2] // kv_width
        inverse = 1.0 / math.sqrt(HD)
        blocks_back = min(8, n_context // 4)
        owned = D // (n_data * n_context)
        member = lax.axis_index("cw")
        chunks = layer_input[0].reshape(tok_rows, n_data, n_cz, n_cw, owned)
        chunks = chunks.transpose(3, 0, 2, 1, 4).reshape(n_cw, tok_rows, n_cz * n_data * owned)
        received = [lax.dynamic_index_in_dim(chunks, member, 0, keepdims=False)]
        for k in range(1, n_cw):
            route = [(i, (i + k) % n_cw) for i in range(n_cw)]
            outgoing = lax.dynamic_index_in_dim(chunks, (member + k) % n_cw, 0, keepdims=False)
            received.append(lax.ppermute(outgoing, "cw", route))
        column_share = jnp.concatenate(received[::-1], axis=0)
        own_pair = jnp.concatenate([keys[0], values[0]], axis=1)
        earlier = [shifted(own_pair, d, n_context) for d in range(blocks_back, 0, -1)]
        window_pair = jnp.concatenate(earlier + [own_pair], axis=0)
        span = window_pair.shape[0]
        key_win = window_pair[:, :kv_width].reshape(span, heads_kv, HD)
        value_win = window_pair[:, kv_width:].reshape(span, heads_kv, HD)
        device = lax.axis_index("cz") * n_cw + lax.axis_index("cw")
        query_pos = device * tok_rows + jnp.arange(tok_rows, dtype=jnp.int32)
        key_pos = (device - blocks_back) * tok_rows + jnp.arange(span, dtype=jnp.int32)
        query_ids = doc_index(doc_lens[0], query_pos)
        key_ids = doc_index(doc_lens[0], key_pos)
        allowed = (
            (key_pos[None, :] <= query_pos[:, None])
            & (key_ids[None, :] == query_ids[:, None])
            & (key_pos[None, :] >= 0)
        )
        query_blk = queries[0].reshape(tok_rows, heads_kv, group, HD)
        grad_blk = out_grad[0].reshape(tok_rows, heads_kv, group, HD)
        scores = (
            jnp.einsum("ighd,jgd->ghij", query_blk, key_win, preferred_element_type=jnp.float32)
            * inverse
        )
        scores = jnp.where(allowed[None, None], scores, NEGATIVE)
        peak = jnp.max(scores, axis=-1, keepdims=True)
        exponent = jnp.exp(scores - peak)
        probs = exponent / jnp.sum(exponent, axis=-1, keepdims=True)
        probs_half = probs.astype(jnp.bfloat16)
        output = jnp.einsum(
            "ghij,jgd->ighd", probs_half, value_win, preferred_element_type=jnp.float32
        )
        out_half = output.astype(jnp.bfloat16)
        delta = jnp.einsum("ighd,ighd->ghi", grad_blk, out_half, preferred_element_type=jnp.float32)
        prob_grad = jnp.einsum(
            "ighd,jgd->ghij", grad_blk, value_win, preferred_element_type=jnp.float32
        )
        score_grad = (probs * (prob_grad - delta[..., None])).astype(jnp.bfloat16)
        query_part = (
            jnp.einsum("ghij,jgd->ighd", score_grad, key_win, preferred_element_type=jnp.float32)
            * inverse
        ).astype(jnp.bfloat16)
        key_part = (
            jnp.einsum("ghij,ighd->jgd", score_grad, query_blk, preferred_element_type=jnp.float32)
            * inverse
        )
        value_part = jnp.einsum(
            "ghij,ighd->jgd", probs_half, grad_blk, preferred_element_type=jnp.float32
        )
        pair_grad = jnp.concatenate(
            [key_part.reshape(span, kv_width), value_part.reshape(span, kv_width)], axis=1
        )

        def block_back(distance):
            first_row = (blocks_back - distance) * tok_rows
            return pair_grad[first_row : first_row + tok_rows]

        total = block_back(0)
        for distance in range(1, blocks_back + 1):
            total = total + shifted(block_back(distance), -distance, n_context)
        pair_half = total.astype(jnp.bfloat16)
        grad_scale = 1.0 / math.sqrt(tok_rows * n_context * n_data)
        group_grad = lax.all_gather(pair_half, "cw", axis=0, tiled=True)
        group_grad = lax.dynamic_slice_in_dim(
            jnp.concatenate([group_grad, group_grad], axis=0),
            (member + 1) % n_cw * tok_rows,
            n_cw * tok_rows,
            0,
        )
        batch_grad = lax.dot_general(
            column_share, group_grad, (((0,), (0,)), ((), ())), preferred_element_type=jnp.float32
        )
        by_layer = lax.psum_scatter(batch_grad * grad_scale, "cz", scatter_dimension=0, tiled=True)
        weight_grad = lax.psum_scatter(by_layer, "dp", scatter_dimension=0, tiled=True)
        attn_out = out_half.reshape(tok_rows, group * kv_width)[None]
        query_grad = query_part.reshape(tok_rows, group * kv_width)[None]
        key_grad = pair_half[:, :kv_width][None]
        value_grad = pair_half[:, kv_width:][None]
        return (attn_out, query_grad, key_grad, value_grad, weight_grad)

    return shards


def solution(mesh):
    n_data = mesh.shape["dp"]
    n_context = mesh.shape["ctx"]
    n_cw = 8 if n_context % 8 == 0 else n_context
    n_cz = n_context // n_cw
    split = Mesh(mesh.devices.reshape(n_data, n_cz, n_cw), ("dp", "cz", "cw"))
    tokens = P("dp", CTX, None)
    in_specs = (tokens, tokens, tokens, tokens, tokens, P("dp", None))
    out_specs = (tokens, tokens, tokens, tokens, P(("dp", "cz", "cw"), None))
    return jax.shard_map(
        make_shards(n_data, n_cz, n_cw),
        mesh=split,
        in_specs=in_specs,
        out_specs=out_specs,
        check_vma=False,
    )
```

profile of v0, /device:TPU:14, one launch (start us, length us, event | category | flops | bytes accessed | tf_op | source)
XLA Modules:
  0.0 378.9 jit_solution(11318091829829404066)
XLA Ops:
  9.4 3.8 collective-permute-start.7
  13.1 3.2 collective-permute-start.6
  16.3 4.0 %collective-permute-start.2 = (bf16[128,1024]{0,1:T(8,128)(2,1)S(1)}, bf16[128,1024]{0,1:T(8,128)(2,1)S(1)}, u32[]{:S(2)}, u32[]{:S(2)}) collective-permute-start(bf16[128,1024]{0,1:T(8,128)(2,1)S(1)} %pad_maximum_fusion.1), channel_id=1, source_target_pairs={{0,6},{1,7},{2,8},{3,9},{4,10},{5,11},{6,12},{7,13},{8,14},{9,15},... | collective-permute-start | bytes 786440 | tf_op jit(solution)/shard_map/ppermute | solution.py:16
  20.3 3.4 collective-permute-start.1
  23.8 4.5 %collective-permute-start = (bf16[128,1024]{0,1:T(8,128)(2,1)S(1)}, bf16[128,1024]{0,1:T(8,128)(2,1)}, u32[]{:S(2)}, u32[]{:S(2)}) collective-permute-start(bf16[128,1024]{0,1:T(8,128)(2,1)S(1)} %pad_maximum_fusion.1), channel_id=1, source_target_pairs={{0,8},{1,9},{2,10},{3,11},{4,12},{5,13},{6,14},{7,15},{8,16},{9,17... | collective-permute-start | bytes 786440 | tf_op jit(solution)/shard_map/ppermute | solution.py:16
  29.4 1.9 and_and_fusion
  31.4 1.4 copy.107
  33.1 3.4 collective-permute-done
  36.6 3.2 collective-permute-start.3
  40.8 8.0 %collective-permute-start.4 = (bf16[128,1024]{0,1:T(8,128)(2,1)S(1)}, bf16[128,1024]{0,1:T(8,128)(2,1)S(1)}, u32[]{:S(2)}, u32[]{:S(2)}) collective-permute-start(bf16[128,1024]{0,1:T(8,128)(2,1)S(1)} %pad_maximum_fusion.1), channel_id=1, source_target_pairs={{0,4},{1,5},{2,6},{3,7},{4,8},{5,9},{6,10},{7,11},{8,12},{9,13},{1... | collective-permute-start | bytes 786440 | tf_op jit(solution)/shard_map/ppermute | solution.py:16
  48.9 8.3 %collective-permute-start.5 = (bf16[128,1024]{0,1:T(8,128)(2,1)S(1)}, bf16[128,1024]{0,1:T(8,128)(2,1)S(1)}, u32[]{:S(2)}, u32[]{:S(2)}) collective-permute-start(bf16[128,1024]{0,1:T(8,128)(2,1)S(1)} %pad_maximum_fusion.1), channel_id=1, source_target_pairs={{0,3},{1,4},{2,5},{3,6},{4,7},{5,8},{6,9},{7,10},{8,11},{9,12},{10... | collective-permute-start | bytes 786440 | tf_op jit(solution)/shard_map/ppermute | solution.py:16
  57.5 3.9 %collective-permute-done.5 = bf16[128,1024]{0,1:T(8,128)(2,1)S(1)} collective-permute-done((bf16[128,1024]{0,1:T(8,128)(2,1)S(1)}, bf16[128,1024]{0,1:T(8,128)(2,1)S(1)}, u32[]{:S(2)}, u32[]{:S(2)}) %collective-permute-start.5) | collective-permute-done | bytes 262176 | tf_op jit(solution)/shard_map/ppermute | solution.py:16
  63.0 6.9 %fusion.42 = (f32[4,5,128]{2,1,0:T(8,128)S(1)}, f32[4,5,128,1152]{2,3,1,0:T(8,128)}) fusion(pred[128,1152]{0,1:T(8,128)(4,1)S(1)} %copy-done.11, bf16[1152,4,128,1]{0,2,3,1:T(8,128)(2,1)S(1)} %bitcast.102, bf16[128,4,5,128]{0,3,2,1:T(8,128)(2,1)S(1)} %bitcast.105), kind=kOutput, calls=%fused_computation.99 | convolution fusion | flops 766772352 | bytes 13789184 | tf_op jit(solution)/shard_map/sub | solution.py:68
  69.9 5.9 %fusion.8 = bf16[4,5,128,1152]{2,3,1,0:T(8,128)(2,1)S(1)} fusion(f32[4,5,128,1152]{2,3,1,0:T(8,128)} %get-tuple-element.51, f32[4,5,128]{2,1,0:T(8,128)S(1)} %get-tuple-element.50), kind=kLoop, calls=%fused_computation.27 | loop fusion | flops 5898240 | bytes 17704960 | tf_op jit(solution)/shard_map/convert_element_type | solution.py:70
  75.8 3.3 fusion.43
  79.0 2.0 copy.114
  81.1 5.2 %fusion.19 = (f32[4,5,128]{2,1,0:T(8,128)S(1)}, bf16[4,128,5,128]{3,1,2,0:T(8,128)(2,1)}) fusion(bf16[4,5,128,128]{2,3,1,0:T(8,128)(2,1)S(1)} %bitcast.98, bf16[1152,4,128,1]{0,2,3,1:T(8,128)(2,1)} %bitcast.100, bf16[4,5,128,1152]{2,3,1,0:T(8,128)(2,1)} %copy-done), kind=kOutput, calls=%fused_computation.40 | convolution fusion | flops 756610560 | bytes 8398848 | tf_op jit(solution)/shard_map/ghij,jgd->ighd/dot_general | solution.py:71
  86.3 5.6 %fusion.3 = bf16[4,5,128,1152]{2,3,1,0:T(8,128)(2,1)S(1)} fusion(bf16[1152,4,128,1]{0,2,3,1:T(8,128)(2,1)S(1)} %bitcast.101, bf16[128,4,5,128]{0,3,2,1:T(8,128)(2,1)S(1)} %bitcast.99, f32[4,5,128]{2,1,0:T(8,128)S(1)} %get-tuple-element.52, f32[4,5,128,1152]{2,3,1,0:T(8,128)} %get-tuple-element.51, f32[4,5,128]{2,1,0:T(8,128)S(1)} %get-tuple-element.50), kind=kOutput, calls=%fused_computation.3 | convolution fusion | flops 766771200 | bytes 19550208 | tf_op jit(solution)/shard_map/ighd,jgd->ghij/dot_general | solution.py:76
  91.9 3.3 fusion.9
  95.2 3.1 copy.113
  98.3 2.0 fusion.30
  100.3 3.7 collective-permute-start.8
  104.1 1.9 collective-permute-start.9
  106.0 2.1 collective-permute-start.10
  108.1 1.3 collective-permute-start.11
  110.7 7.2 %collective-permute-done.8 = f32[128,1024]{1,0:T(8,128)S(1)} collective-permute-done((f32[128,1024]{1,0:T(8,128)S(1)}, f32[128,1024]{1,0:T(8,128)S(1)}, u32[]{:S(2)}, u32[]{:S(2)}) %collective-permute-start.8) | collective-permute-done | bytes 524320 | tf_op jit(solution)/shard_map/ppermute | solution.py:16
  119.3 17.8 %collective-permute-done.9 = f32[128,1024]{1,0:T(8,128)S(1)} collective-permute-done((f32[128,1024]{1,0:T(8,128)S(1)}, f32[128,1024]{1,0:T(8,128)S(1)}, u32[]{:S(2)}, u32[]{:S(2)}) %collective-permute-start.9) | collective-permute-done | bytes 524320 | tf_op jit(solution)/shard_map/ppermute | solution.py:16
  139.6 14.1 %collective-permute-done.11 = f32[128,1024]{1,0:T(8,128)S(1)} collective-permute-done((f32[128,1024]{1,0:T(8,128)S(1)}, f32[128,1024]{1,0:T(8,128)S(1)}, u32[]{:S(2)}, u32[]{:S(2)}) %collective-permute-start.11) | collective-permute-done | bytes 524320 | tf_op jit(solution)/shard_map/ppermute | solution.py:16
  153.8 30.6 %collective-permute-done.12 = f32[128,1024]{1,0:T(8,128)S(1)} collective-permute-done((f32[128,1024]{1,0:T(8,128)S(1)}, f32[128,1024]{1,0:T(8,128)S(1)}, u32[]{:S(2)}, u32[]{:S(2)}) %collective-permute-start.12) | collective-permute-done | bytes 524320 | tf_op jit(solution)/shard_map/ppermute | solution.py:16
  184.3 31.7 %collective-permute-done.13 = f32[128,1024]{1,0:T(8,128)S(1)} collective-permute-done((f32[128,1024]{1,0:T(8,128)S(1)}, f32[128,1024]{1,0:T(8,128)S(1)}, u32[]{:S(2)}, u32[]{:S(2)}) %collective-permute-start.13) | collective-permute-done | bytes 524320 | tf_op jit(solution)/shard_map/ppermute | solution.py:16
  217.4 1.8 copy.115
  219.7 3.6 constant_dynamic-slice_fusion.1
  223.3 1.8 copy.117
  225.1 22.3 %collective-permute-start.16 = (bf16[128,640]{1,0:T(8,128)(2,1)}, bf16[128,640]{1,0:T(8,128)(2,1)S(1)}, u32[]{:S(2)}, u32[]{:S(2)}) collective-permute-start(bf16[128,640]{1,0:T(8,128)(2,1)} %bitcast.36), channel_id=1, source_target_pairs={{0,7},{1,0},{2,1},{3,2},{4,3},{5,4},{6,5},{7,6},{8,15},{9,8},{10,9... | collective-permute-start | bytes 491528 | tf_op jit(solution)/shard_map/ppermute | solution.py:42
  247.3 1.8 copy.118
  249.6 3.0 collective-permute-start.19
  252.7 1.6 collective-permute-start.20
  254.9 2.1 collective-permute-start.21
  257.7 5.9 %collective-permute-done.17 = bf16[128,640]{1,0:T(8,128)(2,1)S(1)} collective-permute-done((bf16[128,640]{1,0:T(8,128)(2,1)}, bf16[128,640]{1,0:T(8,128)(2,1)S(1)}, u32[]{:S(2)}, u32[]{:S(2)}) %collective-permute-start.17) | collective-permute-done | bytes 163872 | tf_op jit(solution)/shard_map/ppermute | solution.py:42
  265.7 4.3 %collective-permute-done.20 = bf16[128,640]{1,0:T(8,128)(2,1)S(1)} collective-permute-done((bf16[128,640]{1,0:T(8,128)(2,1)S(1)}, bf16[128,640]{1,0:T(8,128)(2,1)S(1)}, u32[]{:S(2)}, u32[]{:S(2)}) %collective-permute-start.20) | collective-permute-done | bytes 163872 | tf_op jit(solution)/shard_map/ppermute | solution.py:42
  271.3 1.9 collective-permute-done.22
  274.5 25.8 %all-gather.2.cloned.1.call-done = bf16[1024,1024]{1,0:T(8,128)(2,1)} async-done(((bf16[128,1024]{1,0:T(8,128)(2,1)}), bf16[1024,1024]{1,0:T(8,128)(2,1)}) %all-gather.2.cloned.1.call-update) | async-done | bytes 2097168 | tf_op jit(solution)/shard_map/all_gather | solution.py:104
  300.3 5.1 %fusion.15 = f32[640,1024]{1,0:T(8,128)} fusion(bf16[1024,640]{1,0:T(8,128)(2,1)} %bitcast_dynamic-update-slice_fusion, s32[]{:T(128)S(6)} %select_n.81, bf16[1024,1024]{1,0:T(8,128)(2,1)} %all-gather.2.cloned.1.call-done), kind=kOutput, calls=%fused_computation.35 | convolution fusion | flops 1347026944 | bytes 6029316 | tf_op jit(solution)/shard_map/dot_general | solution.py:111
  307.4 3.9 %fusion.18 = bf16[4,128,5,128]{3,1,2,0:T(8,128)(2,1)S(1)} fusion(bf16[1152,4,128,1]{0,2,3,1:T(8,128)(2,1)S(1)} %bitcast.103, bf16[4,5,128,1152]{2,3,1,0:T(8,128)(2,1)} %copy-done.1), kind=kOutput, calls=%fused_computation.37 | convolution fusion | flops 755630080 | bytes 7733248 | tf_op jit(solution)/shard_map/ghij,jgd->ighd/dot_general | solution.py:81
  313.5 38.7 %reduce-scatter.4.cloned.1.call-done = f32[80,1024]{1,0:T(8,128)} async-done(((f32[640,1024]{1,0:T(8,128)}), f32[80,1024]{1,0:T(8,128)}) %reduce-scatter.4.cloned.1.call-update) | async-done | bytes 327696 | tf_op jit(solution)/shard_map/reduce_scatter | solution.py:114
  352.2 11.9 %fusion = f32[24,1024]{1,0:T(8,128)S(1)} fusion(f32[80,1024]{1,0:T(8,128)} %reduce-scatter.4.cloned.1.call-done), kind=kCustom, calls=%all-reduce-scatter | all-reduce-scatter fusion | flops 98305 | bytes 427008
  364.2 1.9 collective-permute-start.23
  366.8 4.4 %collective-permute-done.23 = f32[12,1024]{1,0:T(8,128)S(1)} collective-permute-done((f32[12,1024]{1,0:T(8,128)S(1)}, f32[12,1024]{1,0:T(8,128)S(1)}, u32[]{:S(2)}, u32[]{:S(2)}) %collective-permute-start.23) | collective-permute-done | bytes 49184
  (96 shorter events, 24.8 us)
Async XLA Ops:
  7.2 25.6 %copy-start.10 = (bf16[1,128,2560]{2,1,0:T(8,128)(2,1)S(1)}, bf16[1,128,2560]{2,1,0:T(8,128)(2,1)}, u32[]{:S(2)}) copy-start(bf16[1,128,2560]{2,1,0:T(8,128)(2,1)} %param.6) | copy-start | bytes 1966084
  7.2 293.1 %all-gather.2.cloned.1.call-start = ((), (), s32[]{:S(2)}) async-start(), calls=%async_computation.1 | async-start | bytes 2359296 | tf_op jit(solution)/shard_map/all_gather | solution.py:104
  9.4 52.2 %collective-permute-start.7 = (bf16[128,1024]{0,1:T(8,128)(2,1)S(1)}, bf16[128,1024]{0,1:T(8,128)(2,1)S(1)}, u32[]{:S(2)}, u32[]{:S(2)}) collective-permute-start(bf16[128,1024]{0,1:T(8,128)(2,1)S(1)} %pad_maximum_fusion.1), channel_id=1, source_target_pairs={{0,1},{1,2},{2,3},{3,4},{4,5},{5,6},{6,7},{7,8},{8,9},{9,10},{10,1... | collective-permute-start | bytes 786440 | tf_op jit(solution)/shard_map/ppermute | solution.py:16
  13.1 48.4 %collective-permute-start.6 = (bf16[128,1024]{0,1:T(8,128)(2,1)S(1)}, bf16[128,1024]{0,1:T(8,128)(2,1)S(1)}, u32[]{:S(2)}, u32[]{:S(2)}) collective-permute-start(bf16[128,1024]{0,1:T(8,128)(2,1)S(1)} %pad_maximum_fusion.1), channel_id=1, source_target_pairs={{0,2},{1,3},{2,4},{3,5},{4,6},{5,7},{6,8},{7,9},{8,10},{9,11},{10,... | collective-permute-start | bytes 786440 | tf_op jit(solution)/shard_map/ppermute | solution.py:16
  16.3 32.6 %collective-permute-start.2 = (bf16[128,1024]{0,1:T(8,128)(2,1)S(1)}, bf16[128,1024]{0,1:T(8,128)(2,1)S(1)}, u32[]{:S(2)}, u32[]{:S(2)}) collective-permute-start(bf16[128,1024]{0,1:T(8,128)(2,1)S(1)} %pad_maximum_fusion.1), channel_id=1, source_target_pairs={{0,6},{1,7},{2,8},{3,9},{4,10},{5,11},{6,12},{7,13},{8,14},{9,15},... | collective-permute-start | bytes 786440 | tf_op jit(solution)/shard_map/ppermute | solution.py:16
  20.3 20.4 %collective-permute-start.1 = (bf16[128,1024]{0,1:T(8,128)(2,1)S(1)}, bf16[128,1024]{0,1:T(8,128)(2,1)S(1)}, u32[]{:S(2)}, u32[]{:S(2)}) collective-permute-start(bf16[128,1024]{0,1:T(8,128)(2,1)S(1)} %pad_maximum_fusion.1), channel_id=1, source_target_pairs={{0,7},{1,8},{2,9},{3,10},{4,11},{5,12},{6,13},{7,14},{8,15},{9,16}... | collective-permute-start | bytes 786440 | tf_op jit(solution)/shard_map/ppermute | solution.py:16
  23.8 12.8 %collective-permute-start = (bf16[128,1024]{0,1:T(8,128)(2,1)S(1)}, bf16[128,1024]{0,1:T(8,128)(2,1)}, u32[]{:S(2)}, u32[]{:S(2)}) collective-permute-start(bf16[128,1024]{0,1:T(8,128)(2,1)S(1)} %pad_maximum_fusion.1), channel_id=1, source_target_pairs={{0,8},{1,9},{2,10},{3,11},{4,12},{5,13},{6,14},{7,15},{8,16},{9,17... | collective-permute-start | bytes 786440 | tf_op jit(solution)/shard_map/ppermute | solution.py:16
  33.1 29.9 %copy-start.7 = (bf16[1,128,2560]{1,2,0:T(8,128)(2,1)}, bf16[1,128,2560]{1,2,0:T(8,128)(2,1)S(1)}, u32[]{:S(2)}) copy-start(bf16[1,128,2560]{1,2,0:T(8,128)(2,1)S(1)} %copy.103) | copy-start | bytes 1966084
  36.6 20.8 %collective-permute-start.3 = (bf16[128,1024]{0,1:T(8,128)(2,1)S(1)}, bf16[128,1024]{0,1:T(8,128)(2,1)S(1)}, u32[]{:S(2)}, u32[]{:S(2)}) collective-permute-start(bf16[128,1024]{0,1:T(8,128)(2,1)S(1)} %pad_maximum_fusion.1), channel_id=1, source_target_pairs={{0,5},{1,6},{2,7},{3,8},{4,9},{5,10},{6,11},{7,12},{8,13},{9,14},{... | collective-permute-start | bytes 786440 | tf_op jit(solution)/shard_map/ppermute | solution.py:16
  40.8 16.6 %collective-permute-start.4 = (bf16[128,1024]{0,1:T(8,128)(2,1)S(1)}, bf16[128,1024]{0,1:T(8,128)(2,1)S(1)}, u32[]{:S(2)}, u32[]{:S(2)}) collective-permute-start(bf16[128,1024]{0,1:T(8,128)(2,1)S(1)} %pad_maximum_fusion.1), channel_id=1, source_target_pairs={{0,4},{1,5},{2,6},{3,7},{4,8},{5,9},{6,10},{7,11},{8,12},{9,13},{1... | collective-permute-start | bytes 786440 | tf_op jit(solution)/shard_map/ppermute | solution.py:16
  48.9 12.5 %collective-permute-start.5 = (bf16[128,1024]{0,1:T(8,128)(2,1)S(1)}, bf16[128,1024]{0,1:T(8,128)(2,1)S(1)}, u32[]{:S(2)}, u32[]{:S(2)}) collective-permute-start(bf16[128,1024]{0,1:T(8,128)(2,1)S(1)} %pad_maximum_fusion.1), channel_id=1, source_target_pairs={{0,3},{1,4},{2,5},{3,6},{4,7},{5,8},{6,9},{7,10},{8,11},{9,12},{10... | collective-permute-start | bytes 786440 | tf_op jit(solution)/shard_map/ppermute | solution.py:16
  61.7 1.3 copy-start.11
  63.0 6.9 %copy-start.4 = (bf16[1152,512]{0,1:T(8,128)(2,1)}, bf16[1152,512]{0,1:T(8,128)(2,1)S(1)}, u32[]{:S(2)}) copy-start(bf16[1152,512]{0,1:T(8,128)(2,1)S(1)} %get-tuple-element.38) | copy-start | bytes 3538948
  75.8 3.3 copy-start
  81.1 5.2 %copy-start.3 = (bf16[1152,512]{0,1:T(8,128)(2,1)S(1)}, bf16[1152,512]{0,1:T(8,128)(2,1)}, u32[]{:S(2)}) copy-start(bf16[1152,512]{0,1:T(8,128)(2,1)} %get-tuple-element.39) | copy-start | bytes 3538948
  86.3 5.6 %copy-start.8 = (bf16[1,128,2560]{1,2,0:T(8,128)(2,1)S(1)}, bf16[1,128,2560]{1,2,0:T(8,128)(2,1)}, u32[]{:S(2)}) copy-start(bf16[1,128,2560]{1,2,0:T(8,128)(2,1)} %copy-done.7) | copy-start | bytes 1966084
  91.9 3.3 copy-start.1
  98.3 117.8 %copy-start.2 = (f32[1152,512]{1,0:T(8,128)S(1)}, f32[1152,512]{1,0:T(8,128)}, u32[]{:S(2)}) copy-start(f32[1152,512]{1,0:T(8,128)} %copy.113) | copy-start | bytes 7077892
  100.3 17.6 %collective-permute-start.8 = (f32[128,1024]{1,0:T(8,128)S(1)}, f32[128,1024]{1,0:T(8,128)S(1)}, u32[]{:S(2)}, u32[]{:S(2)}) collective-permute-start(f32[128,1024]{1,0:T(8,128)S(1)} %get-tuple-element.30), channel_id=1, source_target_pairs={{1,0},{2,1},{3,2},{4,3},{5,4},{6,5},{7,6},{8,7},{9,8},{10,9},{11,1... | collective-permute-start | bytes 1572872 | tf_op jit(solution)/shard_map/ppermute | solution.py:16
  104.1 33.0 %collective-permute-start.9 = (f32[128,1024]{1,0:T(8,128)S(1)}, f32[128,1024]{1,0:T(8,128)S(1)}, u32[]{:S(2)}, u32[]{:S(2)}) collective-permute-start(f32[128,1024]{1,0:T(8,128)S(1)} %get-tuple-element.31), channel_id=1, source_target_pairs={{2,0},{3,1},{4,2},{5,3},{6,4},{7,5},{8,6},{9,7},{10,8},{11,9},{12,... | collective-permute-start | bytes 1572872 | tf_op jit(solution)/shard_map/ppermute | solution.py:16
  106.0 32.3 %collective-permute-start.10 = (f32[128,1024]{1,0:T(8,128)S(1)}, f32[128,1024]{1,0:T(8,128)S(1)}, u32[]{:S(2)}, u32[]{:S(2)}) collective-permute-start(f32[128,1024]{1,0:T(8,128)S(1)} %get-tuple-element.32), channel_id=1, source_target_pairs={{3,0},{4,1},{5,2},{6,3},{7,4},{8,5},{9,6},{10,7},{11,8},{12,9},{13... | collective-permute-start | bytes 1572872 | tf_op jit(solution)/shard_map/ppermute | solution.py:16
  108.1 45.6 %collective-permute-start.11 = (f32[128,1024]{1,0:T(8,128)S(1)}, f32[128,1024]{1,0:T(8,128)S(1)}, u32[]{:S(2)}, u32[]{:S(2)}) collective-permute-start(f32[128,1024]{1,0:T(8,128)S(1)} %get-tuple-element.33), channel_id=1, source_target_pairs={{4,0},{5,1},{6,2},{7,3},{8,4},{9,5},{10,6},{11,7},{12,8},{13,9},{1... | collective-permute-start | bytes 1572872 | tf_op jit(solution)/shard_map/ppermute | solution.py:16
  109.4 74.9 %collective-permute-start.12 = (f32[128,1024]{1,0:T(8,128)S(1)}, f32[128,1024]{1,0:T(8,128)S(1)}, u32[]{:S(2)}, u32[]{:S(2)}) collective-permute-start(f32[128,1024]{1,0:T(8,128)S(1)} %get-tuple-element.34), channel_id=1, source_target_pairs={{5,0},{6,1},{7,2},{8,3},{9,4},{10,5},{11,6},{12,7},{13,8},{14,9},{... | collective-permute-start | bytes 1572872 | tf_op jit(solution)/shard_map/ppermute | solution.py:16
  118.0 98.1 %collective-permute-start.13 = (f32[128,1024]{1,0:T(8,128)S(1)}, f32[128,1024]{1,0:T(8,128)S(1)}, u32[]{:S(2)}, u32[]{:S(2)}) collective-permute-start(f32[128,1024]{1,0:T(8,128)S(1)} %get-tuple-element.35), channel_id=1, source_target_pairs={{6,0},{7,1},{8,2},{9,3},{10,4},{11,5},{12,6},{13,7},{14,8},{15,9},... | collective-permute-start | bytes 1572872 | tf_op jit(solution)/shard_map/ppermute | solution.py:16
  137.0 79.0 %collective-permute-start.15 = (f32[128,1024]{1,0:T(8,128)S(1)}, f32[128,1024]{1,0:T(8,128)S(1)}, u32[]{:S(2)}, u32[]{:S(2)}) collective-permute-start(f32[128,1024]{1,0:T(8,128)S(1)} %get-tuple-element.36), channel_id=1, source_target_pairs={{8,0},{9,1},{10,2},{11,3},{12,4},{13,5},{14,6},{15,7},{16,8},{17,9... | collective-permute-start | bytes 1572872 | tf_op jit(solution)/shard_map/ppermute | solution.py:16
  138.3 77.7 %collective-permute-start.14 = (f32[128,1024]{1,0:T(8,128)S(1)}, f32[128,1024]{1,0:T(8,128)S(1)}, u32[]{:S(2)}, u32[]{:S(2)}) collective-permute-start(f32[128,1024]{1,0:T(8,128)S(1)} %get-tuple-element.37), channel_id=1, source_target_pairs={{7,0},{8,1},{9,2},{10,3},{11,4},{12,5},{13,6},{14,7},{15,8},{16,9}... | collective-permute-start | bytes 1572872 | tf_op jit(solution)/shard_map/ppermute | solution.py:16
  217.2 135.0 %reduce-scatter.4.cloned.1.call-start = ((), (), s32[]{:S(2)}) async-start(), calls=%async_computation.2 | async-start | bytes 2949120 | tf_op jit(solution)/shard_map/reduce_scatter | solution.py:114
  225.1 29.8 %collective-permute-start.16 = (bf16[128,640]{1,0:T(8,128)(2,1)}, bf16[128,640]{1,0:T(8,128)(2,1)S(1)}, u32[]{:S(2)}, u32[]{:S(2)}) collective-permute-start(bf16[128,640]{1,0:T(8,128)(2,1)} %bitcast.36), channel_id=1, source_target_pairs={{0,7},{1,0},{2,1},{3,2},{4,3},{5,4},{6,5},{7,6},{8,15},{9,8},{10,9... | collective-permute-start | bytes 491528 | tf_op jit(solution)/shard_map/ppermute | solution.py:42
  249.1 14.5 %collective-permute-start.17 = (bf16[128,640]{1,0:T(8,128)(2,1)}, bf16[128,640]{1,0:T(8,128)(2,1)S(1)}, u32[]{:S(2)}, u32[]{:S(2)}) collective-permute-start(bf16[128,640]{1,0:T(8,128)(2,1)} %bitcast.37), channel_id=1, source_target_pairs={{0,6},{1,7},{2,0},{3,1},{4,2},{5,3},{6,4},{7,5},{8,14},{9,15},{10,... | collective-permute-start | bytes 491528 | tf_op jit(solution)/shard_map/ppermute | solution.py:42
  249.3 15.0 %collective-permute-start.18 = (bf16[128,640]{1,0:T(8,128)(2,1)S(1)}, bf16[128,640]{1,0:T(8,128)(2,1)S(1)}, u32[]{:S(2)}, u32[]{:S(2)}) collective-permute-start(bf16[128,640]{1,0:T(8,128)(2,1)S(1)} %bitcast.115), channel_id=1, source_target_pairs={{0,5},{1,6},{2,7},{3,0},{4,1},{5,2},{6,3},{7,4},{8,13},{9,14},{10,... | collective-permute-start | bytes 491528 | tf_op jit(solution)/shard_map/ppermute | solution.py:42
  249.6 15.4 %collective-permute-start.19 = (bf16[128,640]{1,0:T(8,128)(2,1)S(1)}, bf16[128,640]{1,0:T(8,128)(2,1)S(1)}, u32[]{:S(2)}, u32[]{:S(2)}) collective-permute-start(bf16[128,640]{1,0:T(8,128)(2,1)S(1)} %bitcast.113), channel_id=1, source_target_pairs={{0,4},{1,5},{2,6},{3,7},{4,0},{5,1},{6,2},{7,3},{8,12},{9,13},{10,... | collective-permute-start | bytes 491528 | tf_op jit(solution)/shard_map/ppermute | solution.py:42
  252.7 17.2 %collective-permute-start.20 = (bf16[128,640]{1,0:T(8,128)(2,1)S(1)}, bf16[128,640]{1,0:T(8,128)(2,1)S(1)}, u32[]{:S(2)}, u32[]{:S(2)}) collective-permute-start(bf16[128,640]{1,0:T(8,128)(2,1)S(1)} %bitcast.112), channel_id=1, source_target_pairs={{0,3},{1,4},{2,5},{3,6},{4,7},{5,0},{6,1},{7,2},{8,11},{9,12},{10,... | collective-permute-start | bytes 491528 | tf_op jit(solution)/shard_map/ppermute | solution.py:42
  254.9 15.7 %collective-permute-start.21 = (bf16[128,640]{1,0:T(8,128)(2,1)S(1)}, bf16[128,640]{1,0:T(8,128)(2,1)S(1)}, u32[]{:S(2)}, u32[]{:S(2)}) collective-permute-start(bf16[128,640]{1,0:T(8,128)(2,1)S(1)} %bitcast.116), channel_id=1, source_target_pairs={{0,2},{1,3},{2,4},{3,5},{4,6},{5,7},{6,0},{7,1},{8,10},{9,11},{10,... | collective-permute-start | bytes 491528 | tf_op jit(solution)/shard_map/ppermute | solution.py:42
  263.6 9.6 %collective-permute-start.22 = (bf16[128,640]{1,0:T(8,128)(2,1)S(1)}, bf16[128,640]{1,0:T(8,128)(2,1)S(1)}, u32[]{:S(2)}, u32[]{:S(2)}) collective-permute-start(bf16[128,640]{1,0:T(8,128)(2,1)S(1)} %bitcast.114), channel_id=1, source_target_pairs={{0,1},{1,2},{2,3},{3,4},{4,5},{5,6},{6,7},{7,0},{8,9},{9,10},{10,1... | collective-permute-start | bytes 491528 | tf_op jit(solution)/shard_map/ppermute | solution.py:42
  305.4 0.7 copy-start.12
  305.4 1.9 copy-start.5
  307.4 5.1 %copy-start.6 = (bf16[4,128,5,128]{3,1,2,0:T(8,128)(2,1)S(1)}, bf16[4,128,5,128]{3,1,2,0:T(8,128)(2,1)}, u32[]{:S(2)}) copy-start(bf16[4,128,5,128]{3,1,2,0:T(8,128)(2,1)} %get-tuple-element.53) | copy-start | bytes 1966084
  311.3 54.8 %copy-start.9 = (bf16[128,1024]{1,0:T(8,128)(2,1)S(1)}, bf16[128,1024]{1,0:T(8,128)(2,1)}, u32[]{:S(2)}) copy-start(bf16[128,1024]{1,0:T(8,128)(2,1)} %fusion.36) | copy-start | bytes 786436
  364.2 7.1 %collective-permute-start.23 = (f32[12,1024]{1,0:T(8,128)S(1)}, f32[12,1024]{1,0:T(8,128)S(1)}, u32[]{:S(2)}, u32[]{:S(2)}) collective-permute-start(f32[12,1024]{1,0:T(8,128)S(1)} %slice.72), channel_id=1, source_target_pairs={{0,64},{64,128},{128,192},{1,65},{65,129},{129,193},{2,66},{66,130... | collective-permute-start | bytes 147464
Sparse Core Ops, SparseCore 0:
  217.4 82.9 all-gather.1
  305.6 46.6 reduce-scatter.3
where the time goes:
time: 380 us; the launch traced here: 379 us
  waiting for transfers between devices  190 us (50%)
  starting transfers between devices  83.7 us (22%)
  local copies, waits for them, and re-layouts  33.4 us (9%)
  matrix products  33.2 us (9%)
  between operations  15.4 us (4%)
  blocking collectives  11.9 us (3%)
  other arithmetic  11.4 us (3%)
    ppermute x16, waiting for transfers between devices, shifted(): return lax.ppermute(block, CTX, route)  109 us
    ppermute x16, starting transfers between devices, shifted(): return lax.ppermute(block, CTX, route)  52.7 us
    reduce_scatter x1, waiting for transfers between devices, shards(): lax.psum_scatter(batch_grad * grad_scale, 'cz', scatter_dimension=0, tile...  38.7 us
    ppermute x7, starting transfers between devices, shards(): received.append(lax.ppermute(outgoing, 'cw', route))  29 us
    all_gather x1, waiting for transfers between devices, shards(): group_grad = lax.all_gather(pair_half, 'cw', axis=0, tiled=True)  25.8 us
    unnamed x52, local copies, waits for them, and re-layouts  16.1 us
    ppermute x7, waiting for transfers between devices, shards(): received.append(lax.ppermute(outgoing, 'cw', route))  12.1 us
    unnamed x1, blocking collectives  11.9 us
  transfers between devices with their start and end apart: 26, of which 13 were waited for; matrix products, arithmetic and copies ran while one was open for 8% of the time, Pallas kernels for 0%

commit v1 on v0

--- a/solution.py
+++ b/solution.py
@@ -101,7 +101,9 @@
             total = total + shifted(block_back(distance), -distance, n_context)
         pair_half = total.astype(jnp.bfloat16)
         grad_scale = 1.0 / math.sqrt(tok_rows * n_context * n_data)
-        group_grad = lax.all_gather(pair_half, "cw", axis=0, tiled=True)
+        group_grad = jnp.concatenate(
+            lax.all_to_all(jnp.stack([pair_half] * lax.axis_size("cw")), "cw", 0, 0), axis=0
+        )
         group_grad = lax.dynamic_slice_in_dim(
             jnp.concatenate([group_grad, group_grad], axis=0),
             (member + 1) % n_cw * tok_rows,

time: 380 us -> 364 us (0.958)
  waiting for transfers between devices: 190 us -> 166 us
  starting transfers between devices: 83.7 us -> 91.7 us
    all_gather x1 -> x0, waiting for transfers between devices: 25.8 us -> none  [shards(): group_grad = lax.all_gather(pair_half, 'cw', axis=0, tiled=True)]
    all_to_all x0 -> x1, starting transfers between devices: none -> 25 us  [shards(): lax.all_to_all(jnp.stack([pair_half] * lax.axis_size('cw')), 'cw', 0, 0)]
    ppermute x7, starting transfers between devices: 29 us -> 12 us  [shards(): received.append(lax.ppermute(outgoing, 'cw', route))]
  transfers between devices with their start and end apart: 26 -> 26, of which waited for: 13 -> 11; matrix products, arithmetic and copies ran while one was open for 8% -> 8% of each run, Pallas kernels for 0% -> 0%
where the time goes in v1:
time: 364 us; the launch traced here: 363 us
  waiting for transfers between devices  166 us (46%)
  starting transfers between devices  91.7 us (25%)
  local copies, waits for them, and re-layouts  34.2 us (9%)
  matrix products  33.3 us (9%)
  between operations  15.2 us (4%)
  blocking collectives  11.5 us (3%)
  other arithmetic  10.8 us (3%)
    ppermute x16, waiting for transfers between devices, shifted(): return lax.ppermute(block, CTX, route)  109 us
    ppermute x16, starting transfers between devices, shifted(): return lax.ppermute(block, CTX, route)  52.7 us
    reduce_scatter x1, waiting for transfers between devices, shards(): lax.psum_scatter(batch_grad * grad_scale, 'cz', scatter_dimension=0, tile...  39.6 us
    all_to_all x1, starting transfers between devices, shards(): lax.all_to_all(jnp.stack([pair_half] * lax.axis_size('cw')), 'cw', 0, 0)  25 us
    unnamed x52, local copies, waits for them, and re-layouts  15.1 us
    ppermute x7, waiting for transfers between devices, shards(): received.append(lax.ppermute(outgoing, 'cw', route))  13.6 us
    ppermute x7, starting transfers between devices, shards(): received.append(lax.ppermute(outgoing, 'cw', route))  12 us
    unnamed x1, blocking collectives  11.5 us
  transfers between devices with their start and end apart: 26, of which 11 were waited for; matrix products, arithmetic and copies ran while one was open for 8% of the time, Pallas kernels for 0%

profile of v1, /device:TPU:14, one launch (start us, length us, event | category | flops | bytes accessed | tf_op | source)
XLA Modules:
  0.0 363.1 jit_solution(13543950536707353296)
XLA Ops:
  9.3 3.8 %collective-permute-start.7 = (bf16[128,1024]{0,1:T(8,128)(2,1)S(1)}, bf16[128,1024]{0,1:T(8,128)(2,1)S(1)}, u32[]{:S(2)}, u32[]{:S(2)}) collective-permute-start(bf16[128,1024]{0,1:T(8,128)(2,1)S(1)} %pad_maximum_fusion.1), channel_id=1, source_target_pairs={{0,1},{1,2},{2,3},{3,4},{4,5},{5,6},{6,7},{7,8},{8,9},{9,10},{10,1... | collective-permute-start | bytes 786440 | tf_op jit(solution)/shard_map/ppermute | solution.py:16
  13.1 3.2 collective-permute-start.6
  16.3 4.0 %collective-permute-start.2 = (bf16[128,1024]{0,1:T(8,128)(2,1)S(1)}, bf16[128,1024]{0,1:T(8,128)(2,1)S(1)}, u32[]{:S(2)}, u32[]{:S(2)}) collective-permute-start(bf16[128,1024]{0,1:T(8,128)(2,1)S(1)} %pad_maximum_fusion.1), channel_id=1, source_target_pairs={{0,6},{1,7},{2,8},{3,9},{4,10},{5,11},{6,12},{7,13},{8,14},{9,15},... | collective-permute-start | bytes 786440 | tf_op jit(solution)/shard_map/ppermute | solution.py:16
  20.3 3.4 collective-permute-start.1
  23.8 4.5 %collective-permute-start = (bf16[128,1024]{0,1:T(8,128)(2,1)S(1)}, bf16[128,1024]{0,1:T(8,128)(2,1)}, u32[]{:S(2)}, u32[]{:S(2)}) collective-permute-start(bf16[128,1024]{0,1:T(8,128)(2,1)S(1)} %pad_maximum_fusion.1), channel_id=1, source_target_pairs={{0,8},{1,9},{2,10},{3,11},{4,12},{5,13},{6,14},{7,15},{8,16},{9,17... | collective-permute-start | bytes 786440 | tf_op jit(solution)/shard_map/ppermute | solution.py:16
  29.4 1.9 and_and_fusion
  31.3 1.4 copy.107
  33.1 3.4 collective-permute-done
  36.5 3.2 collective-permute-start.3
  40.7 8.0 %collective-permute-start.4 = (bf16[128,1024]{0,1:T(8,128)(2,1)S(1)}, bf16[128,1024]{0,1:T(8,128)(2,1)S(1)}, u32[]{:S(2)}, u32[]{:S(2)}) collective-permute-start(bf16[128,1024]{0,1:T(8,128)(2,1)S(1)} %pad_maximum_fusion.1), channel_id=1, source_target_pairs={{0,4},{1,5},{2,6},{3,7},{4,8},{5,9},{6,10},{7,11},{8,12},{9,13},{1... | collective-permute-start | bytes 786440 | tf_op jit(solution)/shard_map/ppermute | solution.py:16
  48.9 8.3 %collective-permute-start.5 = (bf16[128,1024]{0,1:T(8,128)(2,1)S(1)}, bf16[128,1024]{0,1:T(8,128)(2,1)S(1)}, u32[]{:S(2)}, u32[]{:S(2)}) collective-permute-start(bf16[128,1024]{0,1:T(8,128)(2,1)S(1)} %pad_maximum_fusion.1), channel_id=1, source_target_pairs={{0,3},{1,4},{2,5},{3,6},{4,7},{5,8},{6,9},{7,10},{8,11},{9,12},{10... | collective-permute-start | bytes 786440 | tf_op jit(solution)/shard_map/ppermute | solution.py:16
  57.4 3.9 %collective-permute-done.5 = bf16[128,1024]{0,1:T(8,128)(2,1)S(1)} collective-permute-done((bf16[128,1024]{0,1:T(8,128)(2,1)S(1)}, bf16[128,1024]{0,1:T(8,128)(2,1)S(1)}, u32[]{:S(2)}, u32[]{:S(2)}) %collective-permute-start.5) | collective-permute-done | bytes 262176 | tf_op jit(solution)/shard_map/ppermute | solution.py:16
  62.9 6.9 %fusion.42 = (f32[4,5,128]{2,1,0:T(8,128)S(1)}, f32[4,5,128,1152]{2,3,1,0:T(8,128)}) fusion(pred[128,1152]{0,1:T(8,128)(4,1)S(1)} %copy-done.11, bf16[1152,4,128,1]{0,2,3,1:T(8,128)(2,1)S(1)} %bitcast.103, bf16[128,4,5,128]{0,3,2,1:T(8,128)(2,1)S(1)} %bitcast.106), kind=kOutput, calls=%fused_computation.99 | convolution fusion | flops 766772352 | bytes 13789184 | tf_op jit(solution)/shard_map/sub | solution.py:68
  69.8 5.9 %fusion.8 = bf16[4,5,128,1152]{2,3,1,0:T(8,128)(2,1)S(1)} fusion(f32[4,5,128,1152]{2,3,1,0:T(8,128)} %get-tuple-element.51, f32[4,5,128]{2,1,0:T(8,128)S(1)} %get-tuple-element.50), kind=kLoop, calls=%fused_computation.27 | loop fusion | flops 5898240 | bytes 17704960 | tf_op jit(solution)/shard_map/convert_element_type | solution.py:70
  75.7 3.3 fusion.43
  79.0 2.0 copy.114
  81.0 5.2 %fusion.19 = (f32[4,5,128]{2,1,0:T(8,128)S(1)}, bf16[4,128,5,128]{3,1,2,0:T(8,128)(2,1)}) fusion(bf16[4,5,128,128]{2,3,1,0:T(8,128)(2,1)S(1)} %bitcast.99, bf16[1152,4,128,1]{0,2,3,1:T(8,128)(2,1)} %bitcast.101, bf16[4,5,128,1152]{2,3,1,0:T(8,128)(2,1)} %copy-done), kind=kOutput, calls=%fused_computation.40 | convolution fusion | flops 756610560 | bytes 8398848 | tf_op jit(solution)/shard_map/ghij,jgd->ighd/dot_general | solution.py:71
  86.2 5.6 %fusion.3 = bf16[4,5,128,1152]{2,3,1,0:T(8,128)(2,1)S(1)} fusion(bf16[1152,4,128,1]{0,2,3,1:T(8,128)(2,1)S(1)} %bitcast.102, bf16[128,4,5,128]{0,3,2,1:T(8,128)(2,1)S(1)} %bitcast.100, f32[4,5,128]{2,1,0:T(8,128)S(1)} %get-tuple-element.52, f32[4,5,128,1152]{2,3,1,0:T(8,128)} %get-tuple-element.51, f32[4,5,128]{2,1,0:T(8,128)S(1)} %get-tuple-element.50), kind=kOutput, calls=%fused_computation.3 | convolution fusion | flops 766771200 | bytes 19550208 | tf_op jit(solution)/shard_map/ighd,jgd->ghij/dot_general | solution.py:76
  91.9 3.3 fusion.9
  95.1 3.1 copy.113
  98.2 2.0 fusion.30
  100.3 3.8 %collective-permute-start.8 = (f32[128,1024]{1,0:T(8,128)S(1)}, f32[128,1024]{1,0:T(8,128)S(1)}, u32[]{:S(2)}, u32[]{:S(2)}) collective-permute-start(f32[128,1024]{1,0:T(8,128)S(1)} %get-tuple-element.30), channel_id=1, source_target_pairs={{1,0},{2,1},{3,2},{4,3},{5,4},{6,5},{7,6},{8,7},{9,8},{10,9},{11,1... | collective-permute-start | bytes 1572872 | tf_op jit(solution)/shard_map/ppermute | solution.py:16
  104.0 1.9 collective-permute-start.9
  106.0 2.1 collective-permute-start.10
  108.1 1.3 collective-permute-start.11
  109.4 1.3 collective-permute-start.12
  110.7 7.2 %collective-permute-done.8 = f32[128,1024]{1,0:T(8,128)S(1)} collective-permute-done((f32[128,1024]{1,0:T(8,128)S(1)}, f32[128,1024]{1,0:T(8,128)S(1)}, u32[]{:S(2)}, u32[]{:S(2)}) %collective-permute-start.8) | collective-permute-done | bytes 524320 | tf_op jit(solution)/shard_map/ppermute | solution.py:16
  119.2 17.8 %collective-permute-done.9 = f32[128,1024]{1,0:T(8,128)S(1)} collective-permute-done((f32[128,1024]{1,0:T(8,128)S(1)}, f32[128,1024]{1,0:T(8,128)S(1)}, u32[]{:S(2)}, u32[]{:S(2)}) %collective-permute-start.9) | collective-permute-done | bytes 524320 | tf_op jit(solution)/shard_map/ppermute | solution.py:16
  138.3 1.3 collective-permute-start.14
  139.6 14.1 %collective-permute-done.11 = f32[128,1024]{1,0:T(8,128)S(1)} collective-permute-done((f32[128,1024]{1,0:T(8,128)S(1)}, f32[128,1024]{1,0:T(8,128)S(1)}, u32[]{:S(2)}, u32[]{:S(2)}) %collective-permute-start.11) | collective-permute-done | bytes 524320 | tf_op jit(solution)/shard_map/ppermute | solution.py:16
  153.7 30.5 %collective-permute-done.12 = f32[128,1024]{1,0:T(8,128)S(1)} collective-permute-done((f32[128,1024]{1,0:T(8,128)S(1)}, f32[128,1024]{1,0:T(8,128)S(1)}, u32[]{:S(2)}, u32[]{:S(2)}) %collective-permute-start.12) | collective-permute-done | bytes 524320 | tf_op jit(solution)/shard_map/ppermute | solution.py:16
  184.2 31.7 %collective-permute-done.13 = f32[128,1024]{1,0:T(8,128)S(1)} collective-permute-done((f32[128,1024]{1,0:T(8,128)S(1)}, f32[128,1024]{1,0:T(8,128)S(1)}, u32[]{:S(2)}, u32[]{:S(2)}) %collective-permute-start.13) | collective-permute-done | bytes 524320 | tf_op jit(solution)/shard_map/ppermute | solution.py:16
  216.5 1.6 stack.2
  218.1 25.0 %all-to-all-start = ((bf16[8,128,1024]{2,1,0:T(8,128)(2,1)}), bf16[8,128,1024]{2,1,0:T(8,128)(2,1)}, u32[]{:S(2)}, u32[]{:S(2)}) async-start(bf16[8,128,1024]{2,1,0:T(8,128)(2,1)} %stack.2), calls=%async_computation | async-start | bytes 4194304 | tf_op jit(solution)/shard_map/all_to_all | solution.py:105
  244.4 3.6 constant_dynamic-slice_fusion.1
  249.1 1.8 collective-permute-start.16
  250.9 1.8 copy.118
  253.9 3.3 collective-permute-start.18
  257.7 3.0 collective-permute-start.20
  261.2 11.0 %collective-permute-done.16 = bf16[128,640]{1,0:T(8,128)(2,1)S(1)} collective-permute-done((bf16[128,640]{1,0:T(8,128)(2,1)S(1)}, bf16[128,640]{1,0:T(8,128)(2,1)S(1)}, u32[]{:S(2)}, u32[]{:S(2)}) %collective-permute-start.16) | collective-permute-done | bytes 163872 | tf_op jit(solution)/shard_map/ppermute | solution.py:42
  274.1 2.6 collective-permute-done.17
  276.7 2.6 collective-permute-start.22
  284.1 5.1 %fusion.15 = f32[640,1024]{1,0:T(8,128)} fusion(bf16[1024,640]{1,0:T(8,128)(2,1)} %bitcast_dynamic-update-slice_fusion, s32[]{:T(128)S(6)} %select_n.81, bf16[1024,1024]{1,0:T(8,128)(2,1)} %bitcast.44), kind=kOutput, calls=%fused_computation.35 | convolution fusion | flops 1347026944 | bytes 6029316 | tf_op jit(solution)/shard_map/dot_general | solution.py:113
  291.1 3.9 %fusion.18 = bf16[4,128,5,128]{3,1,2,0:T(8,128)(2,1)S(1)} fusion(bf16[1152,4,128,1]{0,2,3,1:T(8,128)(2,1)S(1)} %bitcast.104, bf16[4,5,128,1152]{2,3,1,0:T(8,128)(2,1)} %copy-done.1), kind=kOutput, calls=%fused_computation.37 | convolution fusion | flops 755630080 | bytes 7733248 | tf_op jit(solution)/shard_map/ghij,jgd->ighd/dot_general | solution.py:81
  297.2 39.6 %reduce-scatter.4.cloned.1.call-done = f32[80,1024]{1,0:T(8,128)} async-done(((f32[640,1024]{1,0:T(8,128)}), f32[80,1024]{1,0:T(8,128)}) %reduce-scatter.4.cloned.1.call-update) | async-done | bytes 327696 | tf_op jit(solution)/shard_map/reduce_scatter | solution.py:116
  336.8 11.5 %fusion = f32[24,1024]{1,0:T(8,128)S(1)} fusion(f32[80,1024]{1,0:T(8,128)} %reduce-scatter.4.cloned.1.call-done), kind=kCustom, calls=%all-reduce-scatter | all-reduce-scatter fusion | flops 98305 | bytes 427008
  348.3 1.9 collective-permute-start.23
  350.9 4.4 %collective-permute-done.23 = f32[12,1024]{1,0:T(8,128)S(1)} collective-permute-done((f32[12,1024]{1,0:T(8,128)S(1)}, f32[12,1024]{1,0:T(8,128)S(1)}, u32[]{:S(2)}, u32[]{:S(2)}) %collective-permute-start.23) | collective-permute-done | bytes 49184
  (96 shorter events, 25.5 us)
Async XLA Ops:
  7.2 25.6 %copy-start.10 = (bf16[1,128,2560]{2,1,0:T(8,128)(2,1)S(1)}, bf16[1,128,2560]{2,1,0:T(8,128)(2,1)}, u32[]{:S(2)}) copy-start(bf16[1,128,2560]{2,1,0:T(8,128)(2,1)} %param.6) | copy-start | bytes 1966084
  9.3 52.2 %collective-permute-start.7 = (bf16[128,1024]{0,1:T(8,128)(2,1)S(1)}, bf16[128,1024]{0,1:T(8,128)(2,1)S(1)}, u32[]{:S(2)}, u32[]{:S(2)}) collective-permute-start(bf16[128,1024]{0,1:T(8,128)(2,1)S(1)} %pad_maximum_fusion.1), channel_id=1, source_target_pairs={{0,1},{1,2},{2,3},{3,4},{4,5},{5,6},{6,7},{7,8},{8,9},{9,10},{10,1... | collective-permute-start | bytes 786440 | tf_op jit(solution)/shard_map/ppermute | solution.py:16
  13.1 48.4 %collective-permute-start.6 = (bf16[128,1024]{0,1:T(8,128)(2,1)S(1)}, bf16[128,1024]{0,1:T(8,128)(2,1)S(1)}, u32[]{:S(2)}, u32[]{:S(2)}) collective-permute-start(bf16[128,1024]{0,1:T(8,128)(2,1)S(1)} %pad_maximum_fusion.1), channel_id=1, source_target_pairs={{0,2},{1,3},{2,4},{3,5},{4,6},{5,7},{6,8},{7,9},{8,10},{9,11},{10,... | collective-permute-start | bytes 786440 | tf_op jit(solution)/shard_map/ppermute | solution.py:16
  16.3 32.6 %collective-permute-start.2 = (bf16[128,1024]{0,1:T(8,128)(2,1)S(1)}, bf16[128,1024]{0,1:T(8,128)(2,1)S(1)}, u32[]{:S(2)}, u32[]{:S(2)}) collective-permute-start(bf16[128,1024]{0,1:T(8,128)(2,1)S(1)} %pad_maximum_fusion.1), channel_id=1, source_target_pairs={{0,6},{1,7},{2,8},{3,9},{4,10},{5,11},{6,12},{7,13},{8,14},{9,15},... | collective-permute-start | bytes 786440 | tf_op jit(solution)/shard_map/ppermute | solution.py:16
  20.3 20.4 %collective-permute-start.1 = (bf16[128,1024]{0,1:T(8,128)(2,1)S(1)}, bf16[128,1024]{0,1:T(8,128)(2,1)S(1)}, u32[]{:S(2)}, u32[]{:S(2)}) collective-permute-start(bf16[128,1024]{0,1:T(8,128)(2,1)S(1)} %pad_maximum_fusion.1), channel_id=1, source_target_pairs={{0,7},{1,8},{2,9},{3,10},{4,11},{5,12},{6,13},{7,14},{8,15},{9,16}... | collective-permute-start | bytes 786440 | tf_op jit(solution)/shard_map/ppermute | solution.py:16
  23.8 12.8 %collective-permute-start = (bf16[128,1024]{0,1:T(8,128)(2,1)S(1)}, bf16[128,1024]{0,1:T(8,128)(2,1)}, u32[]{:S(2)}, u32[]{:S(2)}) collective-permute-start(bf16[128,1024]{0,1:T(8,128)(2,1)S(1)} %pad_maximum_fusion.1), channel_id=1, source_target_pairs={{0,8},{1,9},{2,10},{3,11},{4,12},{5,13},{6,14},{7,15},{8,16},{9,17... | collective-permute-start | bytes 786440 | tf_op jit(solution)/shard_map/ppermute | solution.py:16
  33.1 29.9 %copy-start.7 = (bf16[1,128,2560]{1,2,0:T(8,128)(2,1)}, bf16[1,128,2560]{1,2,0:T(8,128)(2,1)S(1)}, u32[]{:S(2)}) copy-start(bf16[1,128,2560]{1,2,0:T(8,128)(2,1)S(1)} %copy.103) | copy-start | bytes 1966084
  36.5 20.8 %collective-permute-start.3 = (bf16[128,1024]{0,1:T(8,128)(2,1)S(1)}, bf16[128,1024]{0,1:T(8,128)(2,1)S(1)}, u32[]{:S(2)}, u32[]{:S(2)}) collective-permute-start(bf16[128,1024]{0,1:T(8,128)(2,1)S(1)} %pad_maximum_fusion.1), channel_id=1, source_target_pairs={{0,5},{1,6},{2,7},{3,8},{4,9},{5,10},{6,11},{7,12},{8,13},{9,14},{... | collective-permute-start | bytes 786440 | tf_op jit(solution)/shard_map/ppermute | solution.py:16
  40.7 16.6 %collective-permute-start.4 = (bf16[128,1024]{0,1:T(8,128)(2,1)S(1)}, bf16[128,1024]{0,1:T(8,128)(2,1)S(1)}, u32[]{:S(2)}, u32[]{:S(2)}) collective-permute-start(bf16[128,1024]{0,1:T(8,128)(2,1)S(1)} %pad_maximum_fusion.1), channel_id=1, source_target_pairs={{0,4},{1,5},{2,6},{3,7},{4,8},{5,9},{6,10},{7,11},{8,12},{9,13},{1... | collective-permute-start | bytes 786440 | tf_op jit(solution)/shard_map/ppermute | solution.py:16
  48.9 12.5 %collective-permute-start.5 = (bf16[128,1024]{0,1:T(8,128)(2,1)S(1)}, bf16[128,1024]{0,1:T(8,128)(2,1)S(1)}, u32[]{:S(2)}, u32[]{:S(2)}) collective-permute-start(bf16[128,1024]{0,1:T(8,128)(2,1)S(1)} %pad_maximum_fusion.1), channel_id=1, source_target_pairs={{0,3},{1,4},{2,5},{3,6},{4,7},{5,8},{6,9},{7,10},{8,11},{9,12},{10... | collective-permute-start | bytes 786440 | tf_op jit(solution)/shard_map/ppermute | solution.py:16
  61.7 1.3 copy-start.11
  62.9 6.9 %copy-start.4 = (bf16[1152,512]{0,1:T(8,128)(2,1)}, bf16[1152,512]{0,1:T(8,128)(2,1)S(1)}, u32[]{:S(2)}) copy-start(bf16[1152,512]{0,1:T(8,128)(2,1)S(1)} %get-tuple-element.38) | copy-start | bytes 3538948
  75.7 3.3 copy-start
  81.0 5.2 %copy-start.3 = (bf16[1152,512]{0,1:T(8,128)(2,1)S(1)}, bf16[1152,512]{0,1:T(8,128)(2,1)}, u32[]{:S(2)}) copy-start(bf16[1152,512]{0,1:T(8,128)(2,1)} %get-tuple-element.39) | copy-start | bytes 3538948
  86.2 5.6 %copy-start.8 = (bf16[1,128,2560]{1,2,0:T(8,128)(2,1)S(1)}, bf16[1,128,2560]{1,2,0:T(8,128)(2,1)}, u32[]{:S(2)}) copy-start(bf16[1,128,2560]{1,2,0:T(8,128)(2,1)} %copy-done.7) | copy-start | bytes 1966084
  91.8 3.3 copy-start.1
  98.2 117.7 %copy-start.2 = (f32[1152,512]{1,0:T(8,128)S(1)}, f32[1152,512]{1,0:T(8,128)}, u32[]{:S(2)}) copy-start(f32[1152,512]{1,0:T(8,128)} %copy.113) | copy-start | bytes 7077892
  100.3 17.6 %collective-permute-start.8 = (f32[128,1024]{1,0:T(8,128)S(1)}, f32[128,1024]{1,0:T(8,128)S(1)}, u32[]{:S(2)}, u32[]{:S(2)}) collective-permute-start(f32[128,1024]{1,0:T(8,128)S(1)} %get-tuple-element.30), channel_id=1, source_target_pairs={{1,0},{2,1},{3,2},{4,3},{5,4},{6,5},{7,6},{8,7},{9,8},{10,9},{11,1... | collective-permute-start | bytes 1572872 | tf_op jit(solution)/shard_map/ppermute | solution.py:16
  104.0 32.9 %collective-permute-start.9 = (f32[128,1024]{1,0:T(8,128)S(1)}, f32[128,1024]{1,0:T(8,128)S(1)}, u32[]{:S(2)}, u32[]{:S(2)}) collective-permute-start(f32[128,1024]{1,0:T(8,128)S(1)} %get-tuple-element.31), channel_id=1, source_target_pairs={{2,0},{3,1},{4,2},{5,3},{6,4},{7,5},{8,6},{9,7},{10,8},{11,9},{12,... | collective-permute-start | bytes 1572872 | tf_op jit(solution)/shard_map/ppermute | solution.py:16
  106.0 32.3 %collective-permute-start.10 = (f32[128,1024]{1,0:T(8,128)S(1)}, f32[128,1024]{1,0:T(8,128)S(1)}, u32[]{:S(2)}, u32[]{:S(2)}) collective-permute-start(f32[128,1024]{1,0:T(8,128)S(1)} %get-tuple-element.32), channel_id=1, source_target_pairs={{3,0},{4,1},{5,2},{6,3},{7,4},{8,5},{9,6},{10,7},{11,8},{12,9},{13... | collective-permute-start | bytes 1572872 | tf_op jit(solution)/shard_map/ppermute | solution.py:16
  108.1 45.6 %collective-permute-start.11 = (f32[128,1024]{1,0:T(8,128)S(1)}, f32[128,1024]{1,0:T(8,128)S(1)}, u32[]{:S(2)}, u32[]{:S(2)}) collective-permute-start(f32[128,1024]{1,0:T(8,128)S(1)} %get-tuple-element.33), channel_id=1, source_target_pairs={{4,0},{5,1},{6,2},{7,3},{8,4},{9,5},{10,6},{11,7},{12,8},{13,9},{1... | collective-permute-start | bytes 1572872 | tf_op jit(solution)/shard_map/ppermute | solution.py:16
  109.4 74.8 %collective-permute-start.12 = (f32[128,1024]{1,0:T(8,128)S(1)}, f32[128,1024]{1,0:T(8,128)S(1)}, u32[]{:S(2)}, u32[]{:S(2)}) collective-permute-start(f32[128,1024]{1,0:T(8,128)S(1)} %get-tuple-element.34), channel_id=1, source_target_pairs={{5,0},{6,1},{7,2},{8,3},{9,4},{10,5},{11,6},{12,7},{13,8},{14,9},{... | collective-permute-start | bytes 1572872 | tf_op jit(solution)/shard_map/ppermute | solution.py:16
  117.9 98.0 %collective-permute-start.13 = (f32[128,1024]{1,0:T(8,128)S(1)}, f32[128,1024]{1,0:T(8,128)S(1)}, u32[]{:S(2)}, u32[]{:S(2)}) collective-permute-start(f32[128,1024]{1,0:T(8,128)S(1)} %get-tuple-element.35), channel_id=1, source_target_pairs={{6,0},{7,1},{8,2},{9,3},{10,4},{11,5},{12,6},{13,7},{14,8},{15,9},... | collective-permute-start | bytes 1572872 | tf_op jit(solution)/shard_map/ppermute | solution.py:16
  137.0 79.0 %collective-permute-start.15 = (f32[128,1024]{1,0:T(8,128)S(1)}, f32[128,1024]{1,0:T(8,128)S(1)}, u32[]{:S(2)}, u32[]{:S(2)}) collective-permute-start(f32[128,1024]{1,0:T(8,128)S(1)} %get-tuple-element.36), channel_id=1, source_target_pairs={{8,0},{9,1},{10,2},{11,3},{12,4},{13,5},{14,6},{15,7},{16,8},{17,9... | collective-permute-start | bytes 1572872 | tf_op jit(solution)/shard_map/ppermute | solution.py:16
  138.3 77.7 %collective-permute-start.14 = (f32[128,1024]{1,0:T(8,128)S(1)}, f32[128,1024]{1,0:T(8,128)S(1)}, u32[]{:S(2)}, u32[]{:S(2)}) collective-permute-start(f32[128,1024]{1,0:T(8,128)S(1)} %get-tuple-element.37), channel_id=1, source_target_pairs={{7,0},{8,1},{9,2},{10,3},{11,4},{12,5},{13,6},{14,7},{15,8},{16,9}... | collective-permute-start | bytes 1572872 | tf_op jit(solution)/shard_map/ppermute | solution.py:16
  218.1 25.0 %copy-start.9 = (bf16[1,128,5120]{2,1,0:T(8,128)(2,1)S(1)}, bf16[1,128,5120]{2,1,0:T(8,128)(2,1)}, u32[]{:S(2)}) copy-start(bf16[1,128,5120]{2,1,0:T(8,128)(2,1)} %param.10) | copy-start | bytes 3932164
  218.1 66.0 %all-to-all-start = ((bf16[8,128,1024]{2,1,0:T(8,128)(2,1)}), bf16[8,128,1024]{2,1,0:T(8,128)(2,1)}, u32[]{:S(2)}, u32[]{:S(2)}) async-start(bf16[8,128,1024]{2,1,0:T(8,128)(2,1)} %stack.2), calls=%async_computation | async-start | bytes 4194304 | tf_op jit(solution)/shard_map/all_to_all | solution.py:105
  243.1 93.7 %reduce-scatter.4.cloned.1.call-start = ((), (), s32[]{:S(2)}) async-start(), calls=%async_computation.2 | async-start | bytes 2949120 | tf_op jit(solution)/shard_map/reduce_scatter | solution.py:116
  249.1 23.1 %collective-permute-start.16 = (bf16[128,640]{1,0:T(8,128)(2,1)S(1)}, bf16[128,640]{1,0:T(8,128)(2,1)S(1)}, u32[]{:S(2)}, u32[]{:S(2)}) collective-permute-start(bf16[128,640]{1,0:T(8,128)(2,1)S(1)} %bitcast.117), channel_id=1, source_target_pairs={{0,7},{1,0},{2,1},{3,2},{4,3},{5,4},{6,5},{7,6},{8,15},{9,8},{10,9... | collective-permute-start | bytes 491528 | tf_op jit(solution)/shard_map/ppermute | solution.py:42
  252.7 23.9 %collective-permute-start.17 = (bf16[128,640]{1,0:T(8,128)(2,1)}, bf16[128,640]{1,0:T(8,128)(2,1)S(1)}, u32[]{:S(2)}, u32[]{:S(2)}) collective-permute-start(bf16[128,640]{1,0:T(8,128)(2,1)} %bitcast.37), channel_id=1, source_target_pairs={{0,6},{1,7},{2,0},{3,1},{4,2},{5,3},{6,4},{7,5},{8,14},{9,15},{10,... | collective-permute-start | bytes 491528 | tf_op jit(solution)/shard_map/ppermute | solution.py:42
  253.9 26.1 %collective-permute-start.18 = (bf16[128,640]{1,0:T(8,128)(2,1)S(1)}, bf16[128,640]{1,0:T(8,128)(2,1)S(1)}, u32[]{:S(2)}, u32[]{:S(2)}) collective-permute-start(bf16[128,640]{1,0:T(8,128)(2,1)S(1)} %bitcast.116), channel_id=1, source_target_pairs={{0,5},{1,6},{2,7},{3,0},{4,1},{5,2},{6,3},{7,4},{8,13},{9,14},{10,... | collective-permute-start | bytes 491528 | tf_op jit(solution)/shard_map/ppermute | solution.py:42
  257.4 23.3 %collective-permute-start.19 = (bf16[128,640]{1,0:T(8,128)(2,1)S(1)}, bf16[128,640]{1,0:T(8,128)(2,1)S(1)}, u32[]{:S(2)}, u32[]{:S(2)}) collective-permute-start(bf16[128,640]{1,0:T(8,128)(2,1)S(1)} %bitcast.114), channel_id=1, source_target_pairs={{0,4},{1,5},{2,6},{3,7},{4,0},{5,1},{6,2},{7,3},{8,12},{9,13},{10,... | collective-permute-start | bytes 491528 | tf_op jit(solution)/shard_map/ppermute | solution.py:42
  257.7 23.7 %collective-permute-start.20 = (bf16[128,640]{1,0:T(8,128)(2,1)S(1)}, bf16[128,640]{1,0:T(8,128)(2,1)S(1)}, u32[]{:S(2)}, u32[]{:S(2)}) collective-permute-start(bf16[128,640]{1,0:T(8,128)(2,1)S(1)} %bitcast.113), channel_id=1, source_target_pairs={{0,3},{1,4},{2,5},{3,6},{4,7},{5,0},{6,1},{7,2},{8,11},{9,12},{10,... | collective-permute-start | bytes 491528 | tf_op jit(solution)/shard_map/ppermute | solution.py:42
  272.3 9.8 %collective-permute-start.21 = (bf16[128,640]{1,0:T(8,128)(2,1)S(1)}, bf16[128,640]{1,0:T(8,128)(2,1)S(1)}, u32[]{:S(2)}, u32[]{:S(2)}) collective-permute-start(bf16[128,640]{1,0:T(8,128)(2,1)S(1)} %bitcast.118), channel_id=1, source_target_pairs={{0,2},{1,3},{2,4},{3,5},{4,6},{5,7},{6,0},{7,1},{8,10},{9,11},{10,... | collective-permute-start | bytes 491528 | tf_op jit(solution)/shard_map/ppermute | solution.py:42
  276.7 6.0 %collective-permute-start.22 = (bf16[128,640]{1,0:T(8,128)(2,1)S(1)}, bf16[128,640]{1,0:T(8,128)(2,1)S(1)}, u32[]{:S(2)}, u32[]{:S(2)}) collective-permute-start(bf16[128,640]{1,0:T(8,128)(2,1)S(1)} %bitcast.115), channel_id=1, source_target_pairs={{0,1},{1,2},{2,3},{3,4},{4,5},{5,6},{6,7},{7,0},{8,9},{9,10},{10,1... | collective-permute-start | bytes 491528 | tf_op jit(solution)/shard_map/ppermute | solution.py:42
  289.2 0.7 copy-start.12
  289.2 1.9 copy-start.5
  291.1 5.0 %copy-start.6 = (bf16[4,128,5,128]{3,1,2,0:T(8,128)(2,1)S(1)}, bf16[4,128,5,128]{3,1,2,0:T(8,128)(2,1)}, u32[]{:S(2)}) copy-start(bf16[4,128,5,128]{3,1,2,0:T(8,128)(2,1)} %get-tuple-element.53) | copy-start | bytes 1966084
  348.3 7.1 %collective-permute-start.23 = (f32[12,1024]{1,0:T(8,128)S(1)}, f32[12,1024]{1,0:T(8,128)S(1)}, u32[]{:S(2)}, u32[]{:S(2)}) collective-permute-start(f32[12,1024]{1,0:T(8,128)S(1)} %slice.72), channel_id=1, source_target_pairs={{0,64},{64,128},{128,192},{1,65},{65,129},{129,193},{2,66},{66,130... | collective-permute-start | bytes 147464
Sparse Core Ops, SparseCore 0:
  289.3 47.4 reduce-scatter.3
